TPU v7x, 32 devices: a whole 2x2x4 slice. The times are simulated.
32 devices in a mesh: occ: 8 (over z, x), aux: 4 (over y, core).
Axes of the slice: x: 2, y: 2, z: 4, core: 2. Of those that a mesh axis runs over, the one named last changes fastest.
Arguments:
- half_integrals: bfloat16 [8, 1024, 1024], P(None, 'aux'), may hold values from -1 to 1
- vir_coef: bfloat16 [1024, 768], P(None, 'occ'), may hold values from -0.1875 to 0.1875
- occ_energy: float32 [8], replicated, may hold values from -3 to -0.3
- vir_energy: float32 [768], replicated, may hold values from 0.1 to 2
Outputs:
- three_index: float32 [1024, 8, 768], P('aux', 'occ')
- vir_density: float32 [768, 768], P(('occ', 'aux'))
All inputs are finite; a program needn't handle non-finite values.
Results may differ from a plain program's by a relative error of at most 0.0006.
The roundings to bfloat16 on the way count: a program that leaves them out, or rounds other values in their place, can miss the bound.
Values may be sent and summed in bfloat16 or wider, within the bound.
A program may use at most 64 MiB of HBM per device.

v0:
```python
import jax
import jax.numpy as jnp
from jax import lax
from jax.sharding import PartitionSpec as P


def from_behind(array, axis, by):
    size = lax.axis_size(axis)
    return lax.ppermute(array, axis, [(i, (i + by) % size) for i in range(size)])


def amplitudes(own_block, own_energy, arrival, arrival_energy, vir_energy, slice_energy):
    coulomb = jnp.einsum("jbp,iap->ijba", arrival, own_block, preferred_element_type=jnp.float32)
    denominator = (
        own_energy[:, None, None, None]
        + arrival_energy[None, :, None, None]
        - slice_energy[None, None, :, None]
        - vir_energy[None, None, None, :]
    )
    return (coulomb / denominator).astype(jnp.bfloat16)


def per_device(half_integrals, vir_coef, occ_energy, vir_energy):
    partial_block = jnp.einsum(
        "ipm,ma->iap", half_integrals, vir_coef, preferred_element_type=jnp.float32
    ).astype(jnp.bfloat16)
    local_block = lax.all_to_all(partial_block, "occ", split_axis=0, concat_axis=1, tiled=True)
    own_block = lax.all_gather(local_block, "aux", axis=2, tiled=True)
    cycle_size = lax.axis_size("occ")
    aux_size = lax.axis_size("aux")
    block_rows, virtuals, aux_total = own_block.shape
    slice_width = virtuals // aux_size
    first_virtual = lax.axis_index("aux") * slice_width
    visitor = lax.dynamic_slice_in_dim(own_block, first_virtual, slice_width, 1)
    slice_energy = lax.dynamic_slice_in_dim(vir_energy, first_virtual, slice_width, 0)
    my_index = lax.axis_index("occ")

    def energy_of(anchor):
        return lax.dynamic_slice_in_dim(occ_energy, anchor % cycle_size * block_rows, block_rows, 0)

    own_energy = energy_of(my_index)
    amp_stack = jnp.zeros((cycle_size, block_rows, block_rows, slice_width, virtuals), jnp.bfloat16)
    store_buffer = jnp.zeros((cycle_size, block_rows, slice_width, aux_total), jnp.bfloat16)

    def absorb(ledger, position, arrival, arrival_energy):
        stacked, keeper = ledger
        amplitude = amplitudes(
            own_block, own_energy, arrival, arrival_energy, vir_energy, slice_energy
        )
        stacked = lax.dynamic_update_index_in_dim(stacked, amplitude, position, 0)
        keeper = lax.dynamic_update_index_in_dim(keeper, arrival, position, 0)
        return (stacked, keeper)

    ledger = absorb((amp_stack, store_buffer), 0, visitor, own_energy)

    def one_turn(turn_index, payload):
        ledger, arrival = payload
        arrival = from_behind(arrival, "occ", 1)
        ledger = absorb(ledger, turn_index, arrival, energy_of(my_index - turn_index))
        return (ledger, arrival)

    ledger, arrival = lax.fori_loop(1, cycle_size, one_turn, (ledger, visitor))
    amp_stack, store_buffer = ledger
    three_index = lax.psum_scatter(
        jnp.einsum("sijba,sjbp->pia", amp_stack, store_buffer, preferred_element_type=jnp.float32),
        "aux",
        scatter_dimension=0,
        tiled=True,
    )
    vir_sum = jnp.einsum(
        "sijca,sijcd->ad", amp_stack, amp_stack, preferred_element_type=jnp.float32
    )
    vir_rows = lax.psum_scatter(vir_sum, ("occ", "aux"), scatter_dimension=0, tiled=True)
    return (three_index, vir_rows / (block_rows * cycle_size * virtuals))


def solution(mesh):
    return jax.shard_map(
        per_device,
        mesh=mesh,
        in_specs=(P(None, "aux", None), P(None, "occ"), P(), P()),
        out_specs=(P("aux", "occ", None), P(("occ", "aux"), None)),
        check_vma=False,
    )
```

profile of v0, /device:TPU:0, one launch (start us, length us, event | category | flops | bytes accessed | tf_op | source)
XLA Modules:
  0.0 311.1 jit_solution(6742861085292702216)
XLA Ops:
  7.2 0.9 copy-done
  8.1 3.6 %fusion.36 = bf16[8,96,256]{2,1,0:T(8,128)(2,1)S(1)} fusion(bf16[8,256,1024]{2,1,0:T(8,128)(2,1)} %param.6, bf16[1024,96]{0,1:T(8,128)(2,1)S(1)} %copy-done), kind=kOutput, calls=%fused_computation.21 | convolution fusion | flops 402849792 | bytes 4784128 | tf_op jit(solution)/shard_map/ipm,ma->iap/dot_general | solution.py:24
  11.7 19.2 %all_to_all.12 = bf16[8,96,256]{2,1,0:T(8,128)(2,1)} all-to-all(bf16[8,96,256]{2,1,0:T(8,128)(2,1)S(1)} %fusion.36), channel_id=1, replica_groups=mesh['occ'=8,'aux'=4] {'occ'}, dimensions={0} | all-to-all | bytes 786432 | tf_op jit(solution)/shard_map/all_to_all | solution.py:27
  31.0 0.6 dynamic_slice.23
  32.7 0.1 broadcast_subtract_fusion.1
  32.8 16.9 %all-gather.2.cloned.1.call-done = bf16[1,768,1024]{2,1,0:T(8,128)(2,1)} async-done(((bf16[1,768,256]{2,1,0:T(8,128)(2,1)}), bf16[1,768,1024]{2,1,0:T(8,128)(2,1)}) %all-gather.2.cloned.1.call-update) | async-done | bytes 1572880 | tf_op jit(solution)/shard_map/all_gather | solution.py:28
  49.6 1.0 constant_dynamic-slice_fusion
  50.7 2.1 fusion.43
  52.8 0.2 dynamic_update_slice.34
  52.9 1.0 fusion.49
  54.0 2.0 dynamic_update_slice.35
  56.0 102.9 %while.21 = (s32[]{:T(128)}, bf16[8,1,1,192,768]{4,3,2,1,0:T(8,128)(2,1)S(1)}, bf16[8,1,192,1024]{3,2,1,0:T(8,128)(2,1)}, bf16[1,192,1024]{2,1,0:T(8,128)(2,1)S(...) while((s32[]{:T(128)}, ...), condition=%wide.region_1.2_spmd, body=%wide.region_0.1_spmd.sunk | while | flops 302432480 | bytes 5413790 | solution.py:62
  56.0 1.5 collective-permute-start
  57.4 0.7 dynamic_slice.30
  59.4 10.6 %collective-permute-done = bf16[1,192,1024]{2,1,0:T(8,128)(2,1)S(1)} collective-permute-done((bf16[1,192,1024]{2,1,0:T(8,128)(2,1)S(1)}, bf16[1,192,1024]{2,1,0:T(8,128)(2,1)S(1)}, u32[]{:S(2)}, u32[]{:S(2)}) %collective-permute-start) | collective-permute-done | bytes 393248 | tf_op jit(solution)/shard_map/while/body/eval_jaxpr/ppermute | solution.py:9
  70.0 0.8 bitcast_dynamic-update-slice_fusion.2
  70.7 2.1 fusion.55
  72.9 0.7 dynamic_slice.30
  74.9 11.2 %collective-permute-done = bf16[1,192,1024]{2,1,0:T(8,128)(2,1)S(1)} collective-permute-done((bf16[1,192,1024]{2,1,0:T(8,128)(2,1)S(1)}, bf16[1,192,1024]{2,1,0:T(8,128)(2,1)S(1)}, u32[]{:S(2)}, u32[]{:S(2)}) %collective-permute-start) | collective-permute-done | bytes 393248 | tf_op jit(solution)/shard_map/while/body/eval_jaxpr/ppermute | solution.py:9
  86.0 0.8 bitcast_dynamic-update-slice_fusion.2
  86.8 2.1 fusion.55
  89.0 0.7 dynamic_slice.30
  90.9 10.3 %collective-permute-done = bf16[1,192,1024]{2,1,0:T(8,128)(2,1)S(1)} collective-permute-done((bf16[1,192,1024]{2,1,0:T(8,128)(2,1)S(1)}, bf16[1,192,1024]{2,1,0:T(8,128)(2,1)S(1)}, u32[]{:S(2)}, u32[]{:S(2)}) %collective-permute-start) | collective-permute-done | bytes 393248 | tf_op jit(solution)/shard_map/while/body/eval_jaxpr/ppermute | solution.py:9
  101.3 0.8 bitcast_dynamic-update-slice_fusion.2
  102.1 2.1 fusion.55
  104.3 0.7 dynamic_slice.30
  106.2 9.4 %collective-permute-done = bf16[1,192,1024]{2,1,0:T(8,128)(2,1)S(1)} collective-permute-done((bf16[1,192,1024]{2,1,0:T(8,128)(2,1)S(1)}, bf16[1,192,1024]{2,1,0:T(8,128)(2,1)S(1)}, u32[]{:S(2)}, u32[]{:S(2)}) %collective-permute-start) | collective-permute-done | bytes 393248 | tf_op jit(solution)/shard_map/while/body/eval_jaxpr/ppermute | solution.py:9
  115.6 0.8 bitcast_dynamic-update-slice_fusion.2
  116.4 2.1 fusion.55
  118.6 0.7 dynamic_slice.30
  120.5 8.6 %collective-permute-done = bf16[1,192,1024]{2,1,0:T(8,128)(2,1)S(1)} collective-permute-done((bf16[1,192,1024]{2,1,0:T(8,128)(2,1)S(1)}, bf16[1,192,1024]{2,1,0:T(8,128)(2,1)S(1)}, u32[]{:S(2)}, u32[]{:S(2)}) %collective-permute-start) | collective-permute-done | bytes 393248 | tf_op jit(solution)/shard_map/while/body/eval_jaxpr/ppermute | solution.py:9
  129.1 0.8 bitcast_dynamic-update-slice_fusion.2
  129.9 2.1 fusion.55
  132.1 0.7 dynamic_slice.30
  134.0 8.5 %collective-permute-done = bf16[1,192,1024]{2,1,0:T(8,128)(2,1)S(1)} collective-permute-done((bf16[1,192,1024]{2,1,0:T(8,128)(2,1)S(1)}, bf16[1,192,1024]{2,1,0:T(8,128)(2,1)S(1)}, u32[]{:S(2)}, u32[]{:S(2)}) %collective-permute-start) | collective-permute-done | bytes 393248 | tf_op jit(solution)/shard_map/while/body/eval_jaxpr/ppermute | solution.py:9
  142.6 0.8 bitcast_dynamic-update-slice_fusion.2
  143.3 2.1 fusion.55
  145.5 0.7 dynamic_slice.30
  147.5 8.5 %collective-permute-done = bf16[1,192,1024]{2,1,0:T(8,128)(2,1)S(1)} collective-permute-done((bf16[1,192,1024]{2,1,0:T(8,128)(2,1)S(1)}, bf16[1,192,1024]{2,1,0:T(8,128)(2,1)S(1)}, u32[]{:S(2)}, u32[]{:S(2)}) %collective-permute-start) | collective-permute-done | bytes 393248 | tf_op jit(solution)/shard_map/while/body/eval_jaxpr/ppermute | solution.py:9
  156.0 0.8 bitcast_dynamic-update-slice_fusion.2
  156.8 2.1 fusion.55
  158.9 1.4 copy-done.2
  160.3 6.1 %fusion.28 = f32[768,768]{1,0:T(8,128)} fusion(bf16[8,1,1,192,768]{4,3,2,1,0:T(8,128)(2,1)} %copy-done.2), kind=kOutput, calls=%fused_computation.16 | convolution fusion | flops 1811939328 | bytes 4718592 | tf_op jit(solution)/shard_map/sijca,sijcd->ad/dot_general | solution.py:70
  166.4 6.0 %fusion.23 = f32[1024,1,768]{2,0,1:T(8,128)} fusion(bf16[8,1,1,192,768]{4,3,2,1,0:T(8,128)(2,1)} %copy-done.2, bf16[8,1,192,1024]{3,2,1,0:T(8,128)(2,1)S(1)} %copy-done.1), kind=kOutput, calls=%fused_computation.15 | convolution fusion | flops 2415919104 | bytes 8650752 | tf_op jit(solution)/shard_map/sijba,sjbp->pia/dot_general | solution.py:65
  172.4 89.9 %reduce-scatter.5.cloned.1.call-done = f32[24,768]{1,0:T(8,128)} async-done(((f32[768,768]{1,0:T(8,128)}), f32[24,768]{1,0:T(8,128)}) %reduce-scatter.5.cloned.1.call-update) | async-done | bytes 73744 | tf_op jit(solution)/shard_map/reduce_scatter | solution.py:73
  262.3 1.5 broadcast_multiply_fusion
  263.9 37.9 %reduce-scatter.3.cloned.1.call-done = f32[256,1,768]{2,0,1:T(8,128)} async-done(((f32[1024,1,768]{2,0,1:T(8,128)}), f32[256,1,768]{2,0,1:T(8,128)}) %reduce-scatter.3.cloned.1.call-update) | async-done | bytes 786448 | tf_op jit(solution)/shard_map/reduce_scatter | solution.py:64
  301.7 2.8 copy.6
  (34 shorter events, 0.8 us)
Async XLA Ops:
  7.2 0.9 copy-start
  7.2 23.9 %copy-start.4 = (f32[8]{0:T(128)S(1)}, f32[8]{0:T(128)}, u32[]{:S(2)}) copy-start(f32[8]{0:T(128)} %param.8) | copy-start | bytes 100
  7.2 25.5 %copy-start.3 = (f32[768]{0:T(1024)S(1)}, f32[768]{0:T(1024)}, u32[]{:S(2)}) copy-start(f32[768]{0:T(1024)} %param.9) | copy-start | bytes 9220
  7.2 42.4 %all-gather.2.cloned.1.call-start = ((), (), s32[]{:S(2)}) async-start(), calls=%async_computation.3 | async-start | bytes 1966080 | tf_op jit(solution)/shard_map/all_gather | solution.py:28
  31.0 231.4 %reduce-scatter.5.cloned.1.call-start = ((), (), s32[]{:S(2)}) async-start(), calls=%async_computation.5 | async-start | bytes 2433024 | tf_op jit(solution)/shard_map/reduce_scatter | solution.py:73
  56.0 14.0 %collective-permute-start = (bf16[1,192,1024]{2,1,0:T(8,128)(2,1)S(1)}, bf16[1,192,1024]{2,1,0:T(8,128)(2,1)S(1)}, u32[]{:S(2)}, u32[]{:S(2)}) collective-permute-start(bf16[1,192,1024]{2,1,0:T(8,128)(2,1)S(1)} %get-tuple-element.424), channel_id=1, source_target_pairs={{0,4},{4,8},{8,12},{12,16},{16,20},{20,24},{24,28},{28,0},{1,5},{5... | collective-permute-start | bytes 1179656 | tf_op jit(solution)/shard_map/while/body/eval_jaxpr/ppermute | solution.py:9
  72.8 13.2 %collective-permute-start = (bf16[1,192,1024]{2,1,0:T(8,128)(2,1)S(1)}, bf16[1,192,1024]{2,1,0:T(8,128)(2,1)S(1)}, u32[]{:S(2)}, u32[]{:S(2)}) collective-permute-start(bf16[1,192,1024]{2,1,0:T(8,128)(2,1)S(1)} %get-tuple-element.424), channel_id=1, source_target_pairs={{0,4},{4,8},{8,12},{12,16},{16,20},{20,24},{24,28},{28,0},{1,5},{5... | collective-permute-start | bytes 1179656 | tf_op jit(solution)/shard_map/while/body/eval_jaxpr/ppermute | solution.py:9
  88.9 12.3 %collective-permute-start = (bf16[1,192,1024]{2,1,0:T(8,128)(2,1)S(1)}, bf16[1,192,1024]{2,1,0:T(8,128)(2,1)S(1)}, u32[]{:S(2)}, u32[]{:S(2)}) collective-permute-start(bf16[1,192,1024]{2,1,0:T(8,128)(2,1)S(1)} %get-tuple-element.424), channel_id=1, source_target_pairs={{0,4},{4,8},{8,12},{12,16},{16,20},{20,24},{24,28},{28,0},{1,5},{5... | collective-permute-start | bytes 1179656 | tf_op jit(solution)/shard_map/while/body/eval_jaxpr/ppermute | solution.py:9
  104.2 11.4 %collective-permute-start = (bf16[1,192,1024]{2,1,0:T(8,128)(2,1)S(1)}, bf16[1,192,1024]{2,1,0:T(8,128)(2,1)S(1)}, u32[]{:S(2)}, u32[]{:S(2)}) collective-permute-start(bf16[1,192,1024]{2,1,0:T(8,128)(2,1)S(1)} %get-tuple-element.424), channel_id=1, source_target_pairs={{0,4},{4,8},{8,12},{12,16},{16,20},{20,24},{24,28},{28,0},{1,5},{5... | collective-permute-start | bytes 1179656 | tf_op jit(solution)/shard_map/while/body/eval_jaxpr/ppermute | solution.py:9
  118.5 10.6 %collective-permute-start = (bf16[1,192,1024]{2,1,0:T(8,128)(2,1)S(1)}, bf16[1,192,1024]{2,1,0:T(8,128)(2,1)S(1)}, u32[]{:S(2)}, u32[]{:S(2)}) collective-permute-start(bf16[1,192,1024]{2,1,0:T(8,128)(2,1)S(1)} %get-tuple-element.424), channel_id=1, source_target_pairs={{0,4},{4,8},{8,12},{12,16},{16,20},{20,24},{24,28},{28,0},{1,5},{5... | collective-permute-start | bytes 1179656 | tf_op jit(solution)/shard_map/while/body/eval_jaxpr/ppermute | solution.py:9
  132.0 10.5 %collective-permute-start = (bf16[1,192,1024]{2,1,0:T(8,128)(2,1)S(1)}, bf16[1,192,1024]{2,1,0:T(8,128)(2,1)S(1)}, u32[]{:S(2)}, u32[]{:S(2)}) collective-permute-start(bf16[1,192,1024]{2,1,0:T(8,128)(2,1)S(1)} %get-tuple-element.424), channel_id=1, source_target_pairs={{0,4},{4,8},{8,12},{12,16},{16,20},{20,24},{24,28},{28,0},{1,5},{5... | collective-permute-start | bytes 1179656 | tf_op jit(solution)/shard_map/while/body/eval_jaxpr/ppermute | solution.py:9
  145.4 10.5 %collective-permute-start = (bf16[1,192,1024]{2,1,0:T(8,128)(2,1)S(1)}, bf16[1,192,1024]{2,1,0:T(8,128)(2,1)S(1)}, u32[]{:S(2)}, u32[]{:S(2)}) collective-permute-start(bf16[1,192,1024]{2,1,0:T(8,128)(2,1)S(1)} %get-tuple-element.424), channel_id=1, source_target_pairs={{0,4},{4,8},{8,12},{12,16},{16,20},{20,24},{24,28},{28,0},{1,5},{5... | collective-permute-start | bytes 1179656 | tf_op jit(solution)/shard_map/while/body/eval_jaxpr/ppermute | solution.py:9
  158.9 1.4 copy-start.2
  160.3 6.1 %copy-start.1 = (bf16[8,1,192,1024]{3,2,1,0:T(8,128)(2,1)S(1)}, bf16[8,1,192,1024]{3,2,1,0:T(8,128)(2,1)}, u32[]{:S(2)}) copy-start(bf16[8,1,192,1024]{3,2,1,0:T(8,128)(2,1)} %get-tuple-element.319) | copy-start | bytes 9437188
  166.4 135.4 %reduce-scatter.3.cloned.1.call-start = ((), (), s32[]{:S(2)}) async-start(), calls=%async_computation.4 | async-start | bytes 3932160 | tf_op jit(solution)/shard_map/reduce_scatter | solution.py:64
Sparse Core Ops, SparseCore 0:
  31.1 18.5 all-gather.1
  166.5 95.8 reduce-scatter.4
  264.9 36.8 reduce-scatter.2
where the time goes:
time: 312 us; the launch traced here: 311 us
  waiting for transfers between devices  212 us (68%)
  matrix products  32.3 us (10%)
  local copies, waits for them, and re-layouts  20.2 us (6%)
  blocking collectives  19.2 us (6%)
  between operations  15 us (5%)
  loops' own time  9.07 us (3%)
    reduce_scatter x1, waiting for transfers between devices, per_device(): lax.psum_scatter(vir_sum, ('occ', 'aux'), scatter_dimension=0, tiled=True)  89.9 us
    ppermute x7, waiting for transfers between devices, from_behind(): lax.ppermute(array, axis, [(i, (i + by) % size) for i in range(size)])  67.1 us
    reduce_scatter x1, waiting for transfers between devices, per_device(): lax.psum_scatter(jnp.einsum('sijba,sjbp->pia', amp_stack, store_buffer, p...  37.9 us
    all_to_all x1, blocking collectives, per_device(): lax.all_to_all(partial_block, 'occ', split_axis=0, concat_axis=1, tiled=T...  19.2 us
    all_gather x1, waiting for transfers between devices, per_device(): own_block = lax.all_gather(local_block, 'aux', axis=2, tiled=True)  16.9 us
    dot_general x8, matrix products, amplitudes(): jnp.einsum('jbp,iap->ijba', arrival, own_block, preferred_element_type=jn...  16.7 us
    another operation x1, loops' own time, per_device(): ledger, arrival = lax.fori_loop(1, cycle_size, one_turn, (ledger, visitor))  9.07 us
    dynamic_update_slice x8, local copies, waits for them, and re-layouts, absorb(): keeper = lax.dynamic_update_index_in_dim(keeper, arrival, position, 0)  7.49 us
  transfers between devices with their start and end apart: 10, of which 10 were waited for; matrix products, arithmetic and copies ran while one was open for 4% of the time, Pallas kernels for 0%

commit v1 on v0

--- a/solution.py
+++ b/solution.py
@@ -24,7 +24,12 @@
     partial_block = jnp.einsum(
         "ipm,ma->iap", half_integrals, vir_coef, preferred_element_type=jnp.float32
     ).astype(jnp.bfloat16)
-    local_block = lax.all_to_all(partial_block, "occ", split_axis=0, concat_axis=1, tiled=True)
+    local_block = jnp.concatenate(
+        lax.all_to_all(
+            jnp.stack(jnp.split(partial_block, lax.axis_size("occ"), axis=0)), "occ", 0, 0
+        ),
+        axis=1,
+    )
     own_block = lax.all_gather(local_block, "aux", axis=2, tiled=True)
     cycle_size = lax.axis_size("occ")
     aux_size = lax.axis_size("aux")

time: 312 us -> 312 us (level)
  no operation moved by 1% of the time
where the time goes in v1:
time: 312 us; the launch traced here: 311 us
  waiting for transfers between devices  212 us (68%)
  matrix products  32.3 us (10%)
  local copies, waits for them, and re-layouts  20.2 us (6%)
  blocking collectives  19.2 us (6%)
  between operations  15 us (5%)
  loops' own time  9.07 us (3%)
    reduce_scatter x1, waiting for transfers between devices, per_device(): lax.psum_scatter(vir_sum, ('occ', 'aux'), scatter_dimension=0, tiled=True)  89.8 us
    ppermute x7, waiting for transfers between devices, from_behind(): lax.ppermute(array, axis, [(i, (i + by) % size) for i in range(size)])  67.1 us
    reduce_scatter x1, waiting for transfers between devices, per_device(): lax.psum_scatter(jnp.einsum('sijba,sjbp->pia', amp_stack, store_buffer, p...  37.9 us
    all_to_all x1, blocking collectives, per_device(): lax.all_to_all(jnp.stack(jnp.split(partial_block, lax.axis_size('occ'), a...  19.2 us
    all_gather x1, waiting for transfers between devices, per_device(): own_block = lax.all_gather(local_block, 'aux', axis=2, tiled=True)  16.9 us
    dot_general x8, matrix products, amplitudes(): jnp.einsum('jbp,iap->ijba', arrival, own_block, preferred_element_type=jn...  16.7 us
    another operation x1, loops' own time, per_device(): ledger, arrival = lax.fori_loop(1, cycle_size, one_turn, (ledger, visitor))  9.07 us
    dynamic_update_slice x8, local copies, waits for them, and re-layouts, absorb(): keeper = lax.dynamic_update_index_in_dim(keeper, arrival, position, 0)  7.49 us
  transfers between devices with their start and end apart: 10, of which 10 were waited for; matrix products, arithmetic and copies ran while one was open for 4% of the time, Pallas kernels for 0%

profile of v1, /device:TPU:0, one launch (start us, length us, event | category | flops | bytes accessed | tf_op | source)
XLA Modules:
  0.0 311.1 jit_solution(7590512767088851178)
XLA Ops:
  7.2 0.9 copy-done
  8.1 3.6 %fusion.36 = bf16[8,96,256]{2,1,0:T(8,128)(2,1)S(1)} fusion(bf16[8,256,1024]{2,1,0:T(8,128)(2,1)} %param.6, bf16[1024,96]{0,1:T(8,128)(2,1)S(1)} %copy-done), kind=kOutput, calls=%fused_computation.21 | convolution fusion | flops 402849792 | bytes 4784128 | tf_op jit(solution)/shard_map/ipm,ma->iap/dot_general | solution.py:24
  11.8 19.2 %all_to_all.5 = bf16[8,1,96,256]{3,2,1,0:T(8,128)(2,1)} all-to-all(bf16[8,1,96,256]{3,2,1,0:T(8,128)(2,1)S(1)} %fusion.48), channel_id=1, replica_groups=mesh['occ'=8,'aux'=4] {'occ'}, dimensions={0} | all-to-all | bytes 786432 | tf_op jit(solution)/shard_map/all_to_all | solution.py:28
  31.1 0.6 dynamic_slice.23
  32.8 0.1 broadcast_subtract_fusion.1
  32.9 16.9 %all-gather.2.cloned.1.call-done = bf16[1,768,1024]{2,1,0:T(8,128)(2,1)} async-done(((bf16[1,768,256]{2,1,0:T(8,128)(2,1)}), bf16[1,768,1024]{2,1,0:T(8,128)(2,1)}) %all-gather.2.cloned.1.call-update) | async-done | bytes 1572880 | tf_op jit(solution)/shard_map/all_gather | solution.py:33
  49.7 1.0 constant_dynamic-slice_fusion
  50.8 2.1 fusion.43
  52.9 0.2 dynamic_update_slice.34
  53.0 1.0 fusion.57
  54.1 2.0 dynamic_update_slice.35
  56.1 102.9 %while.21 = (s32[]{:T(128)}, bf16[8,1,1,192,768]{4,3,2,1,0:T(8,128)(2,1)S(1)}, bf16[8,1,192,1024]{3,2,1,0:T(8,128)(2,1)}, bf16[1,192,1024]{2,1,0:T(8,128)(2,1)S(...) while((s32[]{:T(128)}, ...), condition=%wide.region_1.2_spmd, body=%wide.region_0.1_spmd.sunk | while | flops 302432480 | bytes 5413790 | solution.py:67
  56.1 1.5 collective-permute-start
  57.5 0.7 dynamic_slice.30
  59.5 10.6 %collective-permute-done = bf16[1,192,1024]{2,1,0:T(8,128)(2,1)S(1)} collective-permute-done((bf16[1,192,1024]{2,1,0:T(8,128)(2,1)S(1)}, bf16[1,192,1024]{2,1,0:T(8,128)(2,1)S(1)}, u32[]{:S(2)}, u32[]{:S(2)}) %collective-permute-start) | collective-permute-done | bytes 393248 | tf_op jit(solution)/shard_map/while/body/eval_jaxpr/ppermute | solution.py:9
  70.1 0.8 bitcast_dynamic-update-slice_fusion.2
  70.9 2.1 fusion.63
  73.0 0.7 dynamic_slice.30
  75.0 11.1 %collective-permute-done = bf16[1,192,1024]{2,1,0:T(8,128)(2,1)S(1)} collective-permute-done((bf16[1,192,1024]{2,1,0:T(8,128)(2,1)S(1)}, bf16[1,192,1024]{2,1,0:T(8,128)(2,1)S(1)}, u32[]{:S(2)}, u32[]{:S(2)}) %collective-permute-start) | collective-permute-done | bytes 393248 | tf_op jit(solution)/shard_map/while/body/eval_jaxpr/ppermute | solution.py:9
  86.1 0.8 bitcast_dynamic-update-slice_fusion.2
  86.9 2.1 fusion.63
  89.1 0.7 dynamic_slice.30
  91.0 10.3 %collective-permute-done = bf16[1,192,1024]{2,1,0:T(8,128)(2,1)S(1)} collective-permute-done((bf16[1,192,1024]{2,1,0:T(8,128)(2,1)S(1)}, bf16[1,192,1024]{2,1,0:T(8,128)(2,1)S(1)}, u32[]{:S(2)}, u32[]{:S(2)}) %collective-permute-start) | collective-permute-done | bytes 393248 | tf_op jit(solution)/shard_map/while/body/eval_jaxpr/ppermute | solution.py:9
  101.4 0.8 bitcast_dynamic-update-slice_fusion.2
  102.2 2.1 fusion.63
  104.3 0.7 dynamic_slice.30
  106.3 9.4 %collective-permute-done = bf16[1,192,1024]{2,1,0:T(8,128)(2,1)S(1)} collective-permute-done((bf16[1,192,1024]{2,1,0:T(8,128)(2,1)S(1)}, bf16[1,192,1024]{2,1,0:T(8,128)(2,1)S(1)}, u32[]{:S(2)}, u32[]{:S(2)}) %collective-permute-start) | collective-permute-done | bytes 393248 | tf_op jit(solution)/shard_map/while/body/eval_jaxpr/ppermute | solution.py:9
  115.7 0.8 bitcast_dynamic-update-slice_fusion.2
  116.5 2.1 fusion.63
  118.7 0.7 dynamic_slice.30
  120.6 8.6 %collective-permute-done = bf16[1,192,1024]{2,1,0:T(8,128)(2,1)S(1)} collective-permute-done((bf16[1,192,1024]{2,1,0:T(8,128)(2,1)S(1)}, bf16[1,192,1024]{2,1,0:T(8,128)(2,1)S(1)}, u32[]{:S(2)}, u32[]{:S(2)}) %collective-permute-start) | collective-permute-done | bytes 393248 | tf_op jit(solution)/shard_map/while/body/eval_jaxpr/ppermute | solution.py:9
  129.2 0.8 bitcast_dynamic-update-slice_fusion.2
  130.0 2.1 fusion.63
  132.2 0.7 dynamic_slice.30
  134.1 8.5 %collective-permute-done = bf16[1,192,1024]{2,1,0:T(8,128)(2,1)S(1)} collective-permute-done((bf16[1,192,1024]{2,1,0:T(8,128)(2,1)S(1)}, bf16[1,192,1024]{2,1,0:T(8,128)(2,1)S(1)}, u32[]{:S(2)}, u32[]{:S(2)}) %collective-permute-start) | collective-permute-done | bytes 393248 | tf_op jit(solution)/shard_map/while/body/eval_jaxpr/ppermute | solution.py:9
  142.7 0.8 bitcast_dynamic-update-slice_fusion.2
  143.4 2.1 fusion.63
  145.6 0.7 dynamic_slice.30
  147.5 8.5 %collective-permute-done = bf16[1,192,1024]{2,1,0:T(8,128)(2,1)S(1)} collective-permute-done((bf16[1,192,1024]{2,1,0:T(8,128)(2,1)S(1)}, bf16[1,192,1024]{2,1,0:T(8,128)(2,1)S(1)}, u32[]{:S(2)}, u32[]{:S(2)}) %collective-permute-start) | collective-permute-done | bytes 393248 | tf_op jit(solution)/shard_map/while/body/eval_jaxpr/ppermute | solution.py:9
  156.1 0.8 bitcast_dynamic-update-slice_fusion.2
  156.9 2.1 fusion.63
  159.0 1.4 copy-done.2
  160.4 6.1 %fusion.28 = f32[768,768]{1,0:T(8,128)} fusion(bf16[8,1,1,192,768]{4,3,2,1,0:T(8,128)(2,1)} %copy-done.2), kind=kOutput, calls=%fused_computation.16 | convolution fusion | flops 1811939328 | bytes 4718592 | tf_op jit(solution)/shard_map/sijca,sijcd->ad/dot_general | solution.py:75
  166.5 6.0 %fusion.23 = f32[1024,1,768]{2,0,1:T(8,128)} fusion(bf16[8,1,1,192,768]{4,3,2,1,0:T(8,128)(2,1)} %copy-done.2, bf16[8,1,192,1024]{3,2,1,0:T(8,128)(2,1)S(1)} %copy-done.1), kind=kOutput, calls=%fused_computation.15 | convolution fusion | flops 2415919104 | bytes 8650752 | tf_op jit(solution)/shard_map/sijba,sjbp->pia/dot_general | solution.py:70
  172.5 89.8 %reduce-scatter.5.cloned.1.call-done = f32[24,768]{1,0:T(8,128)} async-done(((f32[768,768]{1,0:T(8,128)}), f32[24,768]{1,0:T(8,128)}) %reduce-scatter.5.cloned.1.call-update) | async-done | bytes 73744 | tf_op jit(solution)/shard_map/reduce_scatter | solution.py:78
  262.4 1.5 broadcast_multiply_fusion
  263.9 37.9 %reduce-scatter.3.cloned.1.call-done = f32[256,1,768]{2,0,1:T(8,128)} async-done(((f32[1024,1,768]{2,0,1:T(8,128)}), f32[256,1,768]{2,0,1:T(8,128)}) %reduce-scatter.3.cloned.1.call-update) | async-done | bytes 786448 | tf_op jit(solution)/shard_map/reduce_scatter | solution.py:69
  301.8 2.8 copy.6
  (42 shorter events, 0.8 us)
Async XLA Ops:
  7.2 0.9 copy-start
  7.2 24.0 %copy-start.4 = (f32[8]{0:T(128)S(1)}, f32[8]{0:T(128)}, u32[]{:S(2)}) copy-start(f32[8]{0:T(128)} %param.8) | copy-start | bytes 100
  7.2 25.6 %copy-start.3 = (f32[768]{0:T(1024)S(1)}, f32[768]{0:T(1024)}, u32[]{:S(2)}) copy-start(f32[768]{0:T(1024)} %param.9) | copy-start | bytes 9220
  7.2 42.5 %all-gather.2.cloned.1.call-start = ((), (), s32[]{:S(2)}) async-start(), calls=%async_computation.3 | async-start | bytes 1966080 | tf_op jit(solution)/shard_map/all_gather | solution.py:33
  31.1 231.3 %reduce-scatter.5.cloned.1.call-start = ((), (), s32[]{:S(2)}) async-start(), calls=%async_computation.5 | async-start | bytes 2433024 | tf_op jit(solution)/shard_map/reduce_scatter | solution.py:78
  56.1 14.0 %collective-permute-start = (bf16[1,192,1024]{2,1,0:T(8,128)(2,1)S(1)}, bf16[1,192,1024]{2,1,0:T(8,128)(2,1)S(1)}, u32[]{:S(2)}, u32[]{:S(2)}) collective-permute-start(bf16[1,192,1024]{2,1,0:T(8,128)(2,1)S(1)} %get-tuple-element.424), channel_id=1, source_target_pairs={{0,4},{4,8},{8,12},{12,16},{16,20},{20,24},{24,28},{28,0},{1,5},{5... | collective-permute-start | bytes 1179656 | tf_op jit(solution)/shard_map/while/body/eval_jaxpr/ppermute | solution.py:9
  73.0 13.2 %collective-permute-start = (bf16[1,192,1024]{2,1,0:T(8,128)(2,1)S(1)}, bf16[1,192,1024]{2,1,0:T(8,128)(2,1)S(1)}, u32[]{:S(2)}, u32[]{:S(2)}) collective-permute-start(bf16[1,192,1024]{2,1,0:T(8,128)(2,1)S(1)} %get-tuple-element.424), channel_id=1, source_target_pairs={{0,4},{4,8},{8,12},{12,16},{16,20},{20,24},{24,28},{28,0},{1,5},{5... | collective-permute-start | bytes 1179656 | tf_op jit(solution)/shard_map/while/body/eval_jaxpr/ppermute | solution.py:9
  89.0 12.3 %collective-permute-start = (bf16[1,192,1024]{2,1,0:T(8,128)(2,1)S(1)}, bf16[1,192,1024]{2,1,0:T(8,128)(2,1)S(1)}, u32[]{:S(2)}, u32[]{:S(2)}) collective-permute-start(bf16[1,192,1024]{2,1,0:T(8,128)(2,1)S(1)} %get-tuple-element.424), channel_id=1, source_target_pairs={{0,4},{4,8},{8,12},{12,16},{16,20},{20,24},{24,28},{28,0},{1,5},{5... | collective-permute-start | bytes 1179656 | tf_op jit(solution)/shard_map/while/body/eval_jaxpr/ppermute | solution.py:9
  104.3 11.4 %collective-permute-start = (bf16[1,192,1024]{2,1,0:T(8,128)(2,1)S(1)}, bf16[1,192,1024]{2,1,0:T(8,128)(2,1)S(1)}, u32[]{:S(2)}, u32[]{:S(2)}) collective-permute-start(bf16[1,192,1024]{2,1,0:T(8,128)(2,1)S(1)} %get-tuple-element.424), channel_id=1, source_target_pairs={{0,4},{4,8},{8,12},{12,16},{16,20},{20,24},{24,28},{28,0},{1,5},{5... | collective-permute-start | bytes 1179656 | tf_op jit(solution)/shard_map/while/body/eval_jaxpr/ppermute | solution.py:9
  118.6 10.6 %collective-permute-start = (bf16[1,192,1024]{2,1,0:T(8,128)(2,1)S(1)}, bf16[1,192,1024]{2,1,0:T(8,128)(2,1)S(1)}, u32[]{:S(2)}, u32[]{:S(2)}) collective-permute-start(bf16[1,192,1024]{2,1,0:T(8,128)(2,1)S(1)} %get-tuple-element.424), channel_id=1, source_target_pairs={{0,4},{4,8},{8,12},{12,16},{16,20},{20,24},{24,28},{28,0},{1,5},{5... | collective-permute-start | bytes 1179656 | tf_op jit(solution)/shard_map/while/body/eval_jaxpr/ppermute | solution.py:9
  132.1 10.5 %collective-permute-start = (bf16[1,192,1024]{2,1,0:T(8,128)(2,1)S(1)}, bf16[1,192,1024]{2,1,0:T(8,128)(2,1)S(1)}, u32[]{:S(2)}, u32[]{:S(2)}) collective-permute-start(bf16[1,192,1024]{2,1,0:T(8,128)(2,1)S(1)} %get-tuple-element.424), channel_id=1, source_target_pairs={{0,4},{4,8},{8,12},{12,16},{16,20},{20,24},{24,28},{28,0},{1,5},{5... | collective-permute-start | bytes 1179656 | tf_op jit(solution)/shard_map/while/body/eval_jaxpr/ppermute | solution.py:9
  145.5 10.5 %collective-permute-start = (bf16[1,192,1024]{2,1,0:T(8,128)(2,1)S(1)}, bf16[1,192,1024]{2,1,0:T(8,128)(2,1)S(1)}, u32[]{:S(2)}, u32[]{:S(2)}) collective-permute-start(bf16[1,192,1024]{2,1,0:T(8,128)(2,1)S(1)} %get-tuple-element.424), channel_id=1, source_target_pairs={{0,4},{4,8},{8,12},{12,16},{16,20},{20,24},{24,28},{28,0},{1,5},{5... | collective-permute-start | bytes 1179656 | tf_op jit(solution)/shard_map/while/body/eval_jaxpr/ppermute | solution.py:9
  159.0 1.4 copy-start.2
  160.4 6.1 %copy-start.1 = (bf16[8,1,192,1024]{3,2,1,0:T(8,128)(2,1)S(1)}, bf16[8,1,192,1024]{3,2,1,0:T(8,128)(2,1)}, u32[]{:S(2)}) copy-start(bf16[8,1,192,1024]{3,2,1,0:T(8,128)(2,1)} %get-tuple-element.319) | copy-start | bytes 9437188
  166.5 135.3 %reduce-scatter.3.cloned.1.call-start = ((), (), s32[]{:S(2)}) async-start(), calls=%async_computation.4 | async-start | bytes 3932160 | tf_op jit(solution)/shard_map/reduce_scatter | solution.py:69
Sparse Core Ops, SparseCore 0:
  31.2 18.5 all-gather.1
  166.6 95.7 reduce-scatter.4
  264.9 36.8 reduce-scatter.2
